TPU v7x, 32 devices: a whole 2x2x4 slice. The times are simulated.
32 devices in a mesh: groups: 2 (over x), dp: 8 (over z, y), mp: 2 (over core).
Axes of the slice: x: 2, y: 2, z: 4, core: 2. Of those that a mesh axis runs over, the one named last changes fastest.
Arguments:
- residual: bfloat16 [48, 128, 8192], P(('groups', 'dp'), None, 'mp'), parts along dimension 0
- lengths: int32 [48], P(('groups', 'dp')), parts along dimension 0, may hold values from 32 to 128
- labels: int32 [48], P(('groups', 'dp')), parts along dimension 0, may hold values from 0 to 1, as said below
- earlier_means: float32 [16, 79, 2, 8192], P(('groups', 'dp'), None, None, 'mp'), parts along dimension 0
- chosen: int32 [2], P('groups'), parts along dimension 0, may hold values from 0 to 79
- norm_gain: float32 [8192], P('mp'), may hold values from 0.1 to 1.9
- key_weight: bfloat16 [2, 4096, 1024], P('mp', 'dp'), may hold values from -0.0625 to 0.0625
- value_weight: bfloat16 [2, 4096, 1024], P('mp', 'dp'), may hold values from -0.0625 to 0.0625
- out_proj: bfloat16 [2, 8192, 8192], P('groups', 'mp', 'dp'), parts along dimension 0
Outputs:
- directions: float32 [160, 8192], P('groups', 'mp'), parts along dimension 0
- key_cache: bfloat16 [48, 128, 1024], P(('groups', 'dp'), None, 'mp'), parts along dimension 0
- value_cache: bfloat16 [48, 128, 1024], P(('groups', 'dp'), None, 'mp'), parts along dimension 0
- ortho_proj: bfloat16 [2, 8192, 8192], P('groups', 'mp', 'dp'), parts along dimension 0
There are 2 independent parts, one for each index of `groups`. A program takes and returns all parts, laid end to end along the dimension named above; an argument that names none is the same for every part. Nothing has to cross between parts.
Inputs may be any that keep to these rules, and one draw needn't show every extreme that they name: Every slab of 3 consecutive prompts holds both labels.
All inputs are finite; a program needn't handle non-finite values.
Results may differ from a plain program's by a relative error of at most 0.0051.
Values may be sent and summed in bfloat16 or wider, within the bound.
A program may use at most 384 MiB of HBM per device.

v0:
```python
import math
import jax
import jax.numpy as jnp
from jax import lax
from jax.sharding import PartitionSpec as P


def direction_parts(residual, lengths, labels, earlier_means, chosen):
    highest = lax.Precision.HIGHEST
    length = residual.shape[1]
    positions = jnp.arange(length, dtype=jnp.int32)
    valid_mask = (positions[None, :] < lengths[:, None]).astype(jnp.bfloat16)
    masked_sums = jnp.einsum("pt,ptd->pd", valid_mask, residual, preferred_element_type=jnp.float32)
    prompt_mean = masked_sums / lengths.astype(jnp.float32)[:, None]
    onehot = (labels[:, None] == jnp.arange(2, dtype=jnp.int32)[None, :]).astype(jnp.float32)
    counts = jnp.sum(onehot, axis=0)
    current = jnp.sum(onehot[:, :, None] * prompt_mean[:, None, :], axis=0) / counts[:, None]
    earlier = earlier_means[0]
    layers = earlier.shape[0] + 1
    picked = lax.dynamic_index_in_dim(
        earlier, jnp.minimum(chosen[0], layers - 2), 0, keepdims=False
    )
    picked = jnp.where(chosen[0] == layers - 1, current, picked)
    weighted, totals = lax.psum((counts[:, None] * picked, counts), "dp")
    merged = weighted / totals[:, None]
    picked_difference = merged[1] - merged[0]
    share = counts / totals
    local = jnp.concatenate(
        [
            share[1] * earlier[:, 1] - share[0] * earlier[:, 0],
            (share[1] * current[1] - share[0] * current[0])[None],
        ],
        axis=0,
    )
    return (picked_difference, local)


def shards(
    residual, lengths, labels, earlier_means, chosen, norm_gain, key_weight, value_weight, out_proj
):
    highest = lax.Precision.HIGHEST
    prompts, length, half_width = residual.shape
    model_width = half_width * lax.axis_size("mp")
    picked_difference, local = direction_parts(residual, lengths, labels, earlier_means, chosen)
    key_full = lax.all_gather(key_weight, "dp", axis=1, tiled=True)[0]
    value_full = lax.all_gather(value_weight, "dp", axis=1, tiled=True)[0]
    difference = lax.psum(local, "dp")
    square_sums = lax.psum(jnp.sum(difference * difference, axis=1), "mp")
    directions = difference * lax.rsqrt(square_sums / model_width + 1e-06)[:, None]
    local_square = jnp.sum(picked_difference * picked_difference)
    local_mean = local_square / half_width + 1e-06
    unit = picked_difference * lax.rsqrt(local_mean)
    token_rows = residual.reshape(prompts * length, half_width)
    row_values = token_rows.astype(jnp.float32)
    matrix = out_proj[0]
    dots = jnp.sum(row_values * unit[None, :], axis=1)
    columns = jnp.sum(matrix.astype(jnp.float32) * unit[:, None], axis=0)
    packed = jnp.concatenate([dots, columns, local_square[None]])
    pieces = lax.all_gather(packed, "mp")
    squares = pieces[:, -1]
    mean_dir = jnp.sum(squares) / model_width + 1e-06
    ratios = jnp.sqrt((squares / half_width + 1e-06) / mean_dir) / math.sqrt(model_width)
    sums = jnp.sum(pieces * ratios[:, None], axis=0)
    projection = sums[: prompts * length]
    column_proj = sums[prompts * length : -1]
    refusal_dir = picked_difference * (lax.rsqrt(mean_dir) / math.sqrt(model_width))
    ablated = row_values - projection[:, None] * refusal_dir[None, :]
    mean_square = lax.psum(jnp.sum(ablated * ablated, axis=1), "mp") / model_width
    normed = (ablated * lax.rsqrt(mean_square + 1e-05)[:, None] * norm_gain[None, :]).astype(
        jnp.bfloat16
    )
    ortho_proj = (matrix.astype(jnp.float32) - refusal_dir[:, None] * column_proj[None, :]).astype(
        jnp.bfloat16
    )[None]
    key_sum = jnp.dot(normed, key_full, preferred_element_type=jnp.float32)
    value_sum = jnp.dot(normed, value_full, preferred_element_type=jnp.float32)
    key_sums, value_sums = (
        lax.psum_scatter(key_sum, "mp", scatter_dimension=1, tiled=True),
        lax.psum_scatter(value_sum, "mp", scatter_dimension=1, tiled=True),
    )
    key_cache = key_sums.astype(jnp.bfloat16).reshape(prompts, length, key_sums.shape[1])
    value_cache = value_sums.astype(jnp.bfloat16).reshape(prompts, length, value_sums.shape[1])
    return (directions, key_cache, value_cache, ortho_proj)


def solution(mesh):
    return jax.shard_map(
        shards,
        mesh=mesh,
        in_specs=(
            P(("groups", "dp"), None, "mp"),
            P(("groups", "dp")),
            P(("groups", "dp")),
            P(("groups", "dp"), None, None, "mp"),
            P("groups"),
            P("mp"),
            P("mp", "dp", None),
            P("mp", "dp", None),
            P("groups", "mp", "dp"),
        ),
        out_specs=(
            P("groups", "mp"),
            P(("groups", "dp"), None, "mp"),
            P(("groups", "dp"), None, "mp"),
            P("groups", "mp", "dp"),
        ),
        check_vma=False,
    )
```

profile of v0, /device:TPU:0, one launch (start us, length us, event | category | flops | bytes accessed | tf_op | source)
XLA Modules:
  0.0 425.7 jit_solution(17136357276199874435)
XLA Ops:
  7.2 0.9 fusion.14
  11.0 4.7 %copy.24 = f32[1,79,2,4096]{3,1,2,0:T(8,128)} copy(f32[1,79,2,4096]{3,2,1,0:T(2,128)} %param.12) | data formatting | bytes 5177344 | tf_op args[3]
  16.4 0.9 fusion.10
  17.3 39.2 %all-reduce.1 = (f32[2]{0:T(128)S(1)}, f32[2,4096]{1,0:T(2,128)S(1)}) all-reduce(f32[2]{0:T(128)S(1)} %fusion.15, f32[2,4096]{1,0:T(2,128)S(1)} %get-tuple-element.10), channel_id=1, replica_groups=mesh['groups'=2,'dp'=8,'mp'=2] {'dp'}, use_global_device_ids=true, to_apply=%region_1.0 | all-reduce | flops 8194 | bytes 65552 | tf_op jit(solution)/shard_map/psum | solution.py:24
  57.0 1.3 fusion.11
  58.4 3.1 fusion.9
  61.5 1.2 pad_maximum_fusion
  67.7 5.1 %fusion.1 = f32[1024]{0:T(1024)S(1)} fusion(bf16[1,4096,1024]{2,1,0:T(8,128)(2,1)} %param.17, f32[4096]{0:T(1024)S(1)} %bitcast.54), kind=kLoop, calls=%fused_computation.3 | loop fusion | flops 12581888 | bytes 8409088 | tf_op jit(solution)/shard_map/reduce_sum | solution.py:57
  72.8 0.8 maximum_dynamic-update-slice_fusion
  73.6 3.3 all-reduce
  78.5 1.2 multiply_reduce_fusion
  79.7 63.7 %all-reduce.5.cloned.1.call-done = f32[80,4096]{1,0:T(8,128)} async-done(((f32[80,4096]{1,0:T(8,128)}), f32[80,4096]{1,0:T(8,128)}) %all-reduce.5.cloned.1.call-update) | async-done | bytes 1310736 | tf_op jit(solution)/shard_map/psum | solution.py:47
  143.4 1.5 multiply_reduce_fusion.1
  144.9 2.5 all-reduce.2
  147.4 3.4 multiply_convert_fusion
  150.8 119.1 %all-gather.4.cloned.1.call-done = bf16[1,4096,1024]{2,1,0:T(8,128)(2,1)} async-done(((bf16[1,512,1024]{2,1,0:T(8,128)(2,1)}), bf16[1,4096,1024]{2,1,0:T(8,128)(2,1)}) %all-gather.4.cloned.1.call-update) | async-done | bytes 8388624 | tf_op jit(solution)/shard_map/all_gather | solution.py:45
  269.9 9.0 %fusion.5 = f32[384,1024]{1,0:T(8,128)} fusion(bf16[384,4096]{1,0:T(8,128)(2,1)} %bitcast.46, bf16[1,4096,1024]{2,1,0:T(8,128)(2,1)} %all-gather.4.cloned.1.call-done), kind=kOutput, calls=%fused_computation.7 | convolution fusion | flops 3221225472 | bytes 13107200 | tf_op jit(solution)/shard_map/dot_general | solution.py:75
  279.0 116.4 %all-gather.6.cloned.1.call-done = bf16[1,4096,1024]{2,1,0:T(8,128)(2,1)} async-done(((bf16[1,512,1024]{2,1,0:T(8,128)(2,1)}), bf16[1,4096,1024]{2,1,0:T(8,128)(2,1)}) %all-gather.6.cloned.1.call-update) | async-done | bytes 8388624 | tf_op jit(solution)/shard_map/all_gather | solution.py:46
  395.4 7.0 %fusion.3 = f32[384,1024]{1,0:T(8,128)} fusion(bf16[384,4096]{1,0:T(8,128)(2,1)S(1)} %bitcast.47, bf16[1,4096,1024]{2,1,0:T(8,128)(2,1)} %all-gather.6.cloned.1.call-done), kind=kOutput, calls=%fused_computation.5 | convolution fusion | flops 3221225472 | bytes 13107200 | tf_op jit(solution)/shard_map/dot_general | solution.py:76
  402.5 8.0 %fusion.2 = bf16[1,4096,1024]{2,1,0:T(8,128)(2,1)} fusion(bf16[1,4096,1024]{2,1,0:T(8,128)(2,1)} %param.17, f32[1024]{0:T(1024)S(1)} %slice.54, f32[4096]{0:T(1024)S(1)} %bitcast.52), kind=kLoop, calls=%fused_computation.4 | loop fusion | flops 16777216 | bytes 16797696 | tf_op jit(solution)/shard_map/convert_element_type | solution.py:72
  410.5 1.2 broadcast_multiply_fusion
  411.7 1.9 convert_element_type.52
  413.7 3.6 reduce-scatter.5.cloned.1.call-done
  417.2 1.9 convert_element_type.53
  (45 shorter events, 8.1 us)
Async XLA Ops:
  7.2 8.5 %copy-start = (bf16[3,128,4096]{2,1,0:T(8,128)(2,1)S(1)}, bf16[3,128,4096]{2,1,0:T(8,128)(2,1)}, u32[]{:S(2)}) copy-start(bf16[3,128,4096]{2,1,0:T(8,128)(2,1)} %param.9) | copy-start | bytes 9437188
  7.2 136.2 %all-reduce.5.cloned.1.call-start = ((), (), s32[]{:S(2)}) async-start(), calls=%async_computation.2 | async-start | bytes 2621440 | tf_op jit(solution)/shard_map/psum | solution.py:47
  61.5 4.2 copy-start.4
  62.7 207.2 %all-gather.4.cloned.1.call-start = ((), (), s32[]{:S(2)}) async-start(), calls=%async_computation.3 | async-start | bytes 9437184 | tf_op jit(solution)/shard_map/all_gather | solution.py:45
  63.5 331.9 %all-gather.6.cloned.1.call-start = ((), (), s32[]{:S(2)}) async-start(), calls=%async_computation.5 | async-start | bytes 9437184 | tf_op jit(solution)/shard_map/all_gather | solution.py:46
  64.2 347.5 %reduce-scatter.3.cloned.1.call-start = ((), (), s32[]{:S(2)}) async-start(), calls=%async_computation.4 | async-start | bytes 2359296 | tf_op jit(solution)/shard_map/reduce_scatter | solution.py:78
  72.8 74.6 %copy-start.3 = (f32[4096]{0:T(1024)S(1)}, f32[4096]{0:T(1024)}, u32[]{:S(2)}) copy-start(f32[4096]{0:T(1024)} %param.14) | copy-start | bytes 49156
  269.9 125.5 %copy-start.2 = (bf16[3,128,4096]{2,1,0:T(8,128)(2,1)S(1)}, bf16[3,128,4096]{2,1,0:T(8,128)(2,1)}, u32[]{:S(2)}) copy-start(bf16[3,128,4096]{2,1,0:T(8,128)(2,1)} %multiply_convert_fusion) | copy-start | bytes 9437188
  279.0 138.3 %reduce-scatter.5.cloned.1.call-start = ((), (), s32[]{:S(2)}) async-start(), calls=%async_computation.6 | async-start | bytes 2359296 | tf_op jit(solution)/shard_map/reduce_scatter | solution.py:79
  402.4 8.0 %copy-start.1 = (f32[80,4096]{1,0:T(8,128)S(1)}, f32[80,4096]{1,0:T(8,128)}, u32[]{:S(2)}) copy-start(f32[80,4096]{1,0:T(8,128)} %all-reduce.5.cloned.1.call-done) | copy-start | bytes 3932164
Sparse Core Ops, SparseCore 0:
  62.8 80.5 all-reduce.4
  145.7 124.1 all-gather.3
  272.2 123.1 all-gather.5
  397.6 7.2 reduce-scatter.2
  406.9 10.2 reduce-scatter.4
where the time goes:
time: 426 us
  waiting for transfers between devices  304 us (71%)
  blocking collectives  44.9 us (11%)
  other arithmetic  37 us (9%)
  between operations  16.7 us (4%)
  matrix products  16.6 us (4%)
  local copies, waits for them, and re-layouts  6.11 us (1%)
    all_gather x1, waiting for transfers between devices, shards(): key_full = lax.all_gather(key_weight, 'dp', axis=1, tiled=True)[0]  119 us
    all_gather x1, waiting for transfers between devices, shards(): value_full = lax.all_gather(value_weight, 'dp', axis=1, tiled=True)[0]  116 us
    psum x1, waiting for transfers between devices, shards(): difference = lax.psum(local, 'dp')  63.7 us
    psum x1, blocking collectives, direction_parts(): weighted, totals = lax.psum((counts[:, None] * picked, counts), 'dp')  39.2 us
    dot_general x1, matrix products, shards(): key_sum = jnp.dot(normed, key_full, preferred_element_type=jnp.float32)  9.04 us
  transfers between devices with their start and end apart: 5, of which 4 were waited for; matrix products, arithmetic and copies ran while one was open for 10% of the time, Pallas kernels for 0%

commit v1 on v0

--- a/solution.py
+++ b/solution.py
@@ -3,6 +3,8 @@
 import jax.numpy as jnp
 from jax import lax
 from jax.sharding import PartitionSpec as P
+
+lead_limits_up = lambda local_x: lax.all_gather(local_x, "dp").sum(axis=0)
 
 
 def direction_parts(residual, lengths, labels, earlier_means, chosen):
@@ -44,7 +46,7 @@
     picked_difference, local = direction_parts(residual, lengths, labels, earlier_means, chosen)
     key_full = lax.all_gather(key_weight, "dp", axis=1, tiled=True)[0]
     value_full = lax.all_gather(value_weight, "dp", axis=1, tiled=True)[0]
-    difference = lax.psum(local, "dp")
+    difference = lead_limits_up(local)
     square_sums = lax.psum(jnp.sum(difference * difference, axis=1), "mp")
     directions = difference * lax.rsqrt(square_sums / model_width + 1e-06)[:, None]
     local_square = jnp.sum(picked_difference * picked_difference)

time: 426 us -> 489 us (1.15)
  waiting for transfers between devices: 304 us -> 364 us
  other arithmetic: 37 us -> 42.8 us
    all_gather x0 -> x1, waiting for transfers between devices: none -> 130 us  [lead_limits_up = lambda local_x: lax.all_gather(local_x, 'dp').sum(axis=0)]
    psum x1 -> x0, waiting for transfers between devices: 63.7 us -> none  [shards(): difference = lax.psum(local, 'dp')]
    all_gather x1, waiting for transfers between devices: 119 us -> 112 us  [shards(): key_full = lax.all_gather(key_weight, 'dp', axis=1, tiled=True)[0]]
    reduce_sum x0 -> x1, other arithmetic: none -> 5.87 us  [lead_limits_up = lambda local_x: lax.all_gather(local_x, 'dp').sum(axis=0)]
where the time goes in v1:
time: 489 us
  waiting for transfers between devices  364 us (74%)
  blocking collectives  45.1 us (9%)
  other arithmetic  42.8 us (9%)
  matrix products  18.4 us (4%)
  between operations  16.7 us (3%)
    all_gather x1, waiting for transfers between devices, lead_limits_up = lambda local_x: lax.all_gather(local_x, 'dp').sum(axis=0)  130 us
    all_gather x1, waiting for transfers between devices, shards(): value_full = lax.all_gather(value_weight, 'dp', axis=1, tiled=True)[0]  116 us
    all_gather x1, waiting for transfers between devices, shards(): key_full = lax.all_gather(key_weight, 'dp', axis=1, tiled=True)[0]  112 us
    psum x1, blocking collectives, direction_parts(): weighted, totals = lax.psum((counts[:, None] * picked, counts), 'dp')  39.2 us
  transfers between devices with their start and end apart: 5, of which 4 were waited for; matrix products, arithmetic and copies ran while one was open for 10% of the time, Pallas kernels for 0%

profile of v1, /device:TPU:0, one launch (start us, length us, event | category | flops | bytes accessed | tf_op | source)
XLA Modules:
  0.0 488.9 jit_solution(15337276349135342574)
XLA Ops:
  7.2 0.9 fusion.13
  10.9 2.4 fusion.11
  13.7 39.2 %all-reduce.1 = (f32[2]{0:T(128)S(1)}, f32[2,4096]{1,0:T(2,128)S(1)}) all-reduce(f32[2]{0:T(128)S(1)} %fusion.14, f32[2,4096]{1,0:T(2,128)S(1)} %get-tuple-element.10), channel_id=1, replica_groups=mesh['groups'=2,'dp'=8,'mp'=2] {'dp'}, use_global_device_ids=true, to_apply=%region_1.0 | all-reduce | flops 8194 | bytes 65552 | tf_op jit(solution)/shard_map/psum | solution.py:26
  53.4 1.3 fusion.10
  54.8 3.0 fusion.8
  57.7 0.8 copy.21
  58.6 1.2 pad_maximum_fusion
  64.7 5.9 %fusion.1 = f32[1024]{0:T(1024)S(1)} fusion(bf16[1,4096,1024]{2,1,0:T(8,128)(2,1)} %param.17, f32[4096]{0:T(1024)S(1)} %bitcast.56), kind=kLoop, calls=%fused_computation.3 | loop fusion | flops 12581888 | bytes 8409088 | tf_op jit(solution)/shard_map/reduce_sum | solution.py:59
  71.5 3.3 all-reduce
  76.4 1.2 multiply_reduce_fusion
  77.6 130.5 %all-gather.10.cloned.1.call-done = f32[640,4096]{1,0:T(8,128)} async-done(((f32[80,4096]{1,0:T(8,128)}), f32[640,4096]{1,0:T(8,128)}) %all-gather.10.cloned.1.call-update) | async-done | bytes 10485776 | tf_op jit(solution)/shard_map/all_gather | solution.py:7
  208.0 5.9 %reduce_sum.96 = f32[80,4096]{1,0:T(8,128)} reduce(f32[8,80,4096]{2,1,0:T(8,128)} %bitcast.45, f32[]{:T(128)} %constant.12.clone.1), dimensions={0}, to_apply=%region_3.4 | reduce | flops 2293760 | bytes 11796484 | tf_op jit(solution)/shard_map/reduce_sum | solution.py:7
  213.9 1.5 multiply_reduce_fusion.1
  215.4 2.7 all-reduce.2
  218.1 3.4 multiply_convert_fusion
  221.5 111.9 %all-gather.6.cloned.1.call-done = bf16[1,4096,1024]{2,1,0:T(8,128)(2,1)} async-done(((bf16[1,512,1024]{2,1,0:T(8,128)(2,1)}), bf16[1,4096,1024]{2,1,0:T(8,128)(2,1)}) %all-gather.6.cloned.1.call-update) | async-done | bytes 8388624 | tf_op jit(solution)/shard_map/all_gather | solution.py:47
  333.3 9.0 %fusion.5 = f32[384,1024]{1,0:T(8,128)} fusion(bf16[384,4096]{1,0:T(8,128)(2,1)} %bitcast.47, bf16[1,4096,1024]{2,1,0:T(8,128)(2,1)} %all-gather.6.cloned.1.call-done), kind=kOutput, calls=%fused_computation.7 | convolution fusion | flops 3221225472 | bytes 13107200 | tf_op jit(solution)/shard_map/dot_general | solution.py:77
  342.4 116.2 %all-gather.8.cloned.1.call-done = bf16[1,4096,1024]{2,1,0:T(8,128)(2,1)} async-done(((bf16[1,512,1024]{2,1,0:T(8,128)(2,1)}), bf16[1,4096,1024]{2,1,0:T(8,128)(2,1)}) %all-gather.8.cloned.1.call-update) | async-done | bytes 8388624 | tf_op jit(solution)/shard_map/all_gather | solution.py:48
  458.6 6.9 %fusion.3 = f32[384,1024]{1,0:T(8,128)} fusion(bf16[384,4096]{1,0:T(8,128)(2,1)S(1)} %bitcast.48, bf16[1,4096,1024]{2,1,0:T(8,128)(2,1)} %all-gather.8.cloned.1.call-done), kind=kOutput, calls=%fused_computation.5 | convolution fusion | flops 3221225472 | bytes 13107200 | tf_op jit(solution)/shard_map/dot_general | solution.py:78
  465.6 8.0 %fusion.2 = bf16[1,4096,1024]{2,1,0:T(8,128)(2,1)} fusion(bf16[1,4096,1024]{2,1,0:T(8,128)(2,1)} %param.17, f32[1024]{0:T(1024)S(1)} %slice.54, f32[4096]{0:T(1024)S(1)} %bitcast.54), kind=kLoop, calls=%fused_computation.4 | loop fusion | flops 16777216 | bytes 16797696 | tf_op jit(solution)/shard_map/convert_element_type | solution.py:74
  473.6 1.2 broadcast_multiply_fusion
  474.8 1.9 convert_element_type.52
  476.8 3.7 reduce-scatter.5.cloned.1.call-done
  480.4 1.9 convert_element_type.53
  (48 shorter events, 8.5 us)
Async XLA Ops:
  7.2 6.4 %copy-start.3 = (f32[1,79,2,4096]{3,2,1,0:T(2,128)S(1)}, f32[1,79,2,4096]{3,2,1,0:T(2,128)}, u32[]{:S(2)}) copy-start(f32[1,79,2,4096]{3,2,1,0:T(2,128)} %param.12) | copy-start | bytes 7766020
  7.2 200.9 %all-gather.10.cloned.1.call-start = ((), (), s32[]{:S(2)}) async-start(), calls=%async_computation.6 | async-start | bytes 11796480 | tf_op jit(solution)/shard_map/all_gather | solution.py:7
  58.6 4.2 copy-start.5
  58.6 5.4 %copy-start = (bf16[3,128,4096]{2,1,0:T(8,128)(2,1)S(1)}, bf16[3,128,4096]{2,1,0:T(8,128)(2,1)}, u32[]{:S(2)}) copy-start(bf16[3,128,4096]{2,1,0:T(8,128)(2,1)} %param.9) | copy-start | bytes 9437188
  59.8 273.5 %all-gather.6.cloned.1.call-start = ((), (), s32[]{:S(2)}) async-start(), calls=%async_computation.2 | async-start | bytes 9437184 | tf_op jit(solution)/shard_map/all_gather | solution.py:47
  60.5 398.1 %all-gather.8.cloned.1.call-start = ((), (), s32[]{:S(2)}) async-start(), calls=%async_computation.4 | async-start | bytes 9437184 | tf_op jit(solution)/shard_map/all_gather | solution.py:48
  61.3 413.6 %reduce-scatter.3.cloned.1.call-start = ((), (), s32[]{:S(2)}) async-start(), calls=%async_computation.3 | async-start | bytes 2359296 | tf_op jit(solution)/shard_map/reduce_scatter | solution.py:80
  208.0 10.0 %copy-start.4 = (f32[4096]{0:T(1024)S(1)}, f32[4096]{0:T(1024)}, u32[]{:S(2)}) copy-start(f32[4096]{0:T(1024)} %param.14) | copy-start | bytes 49156
  333.3 125.3 %copy-start.2 = (bf16[3,128,4096]{2,1,0:T(8,128)(2,1)S(1)}, bf16[3,128,4096]{2,1,0:T(8,128)(2,1)}, u32[]{:S(2)}) copy-start(bf16[3,128,4096]{2,1,0:T(8,128)(2,1)} %multiply_convert_fusion) | copy-start | bytes 9437188
  342.4 138.1 %reduce-scatter.5.cloned.1.call-start = ((), (), s32[]{:S(2)}) async-start(), calls=%async_computation.5 | async-start | bytes 2359296 | tf_op jit(solution)/shard_map/reduce_scatter | solution.py:81
  465.6 8.0 %copy-start.1 = (f32[80,4096]{1,0:T(8,128)S(1)}, f32[80,4096]{1,0:T(8,128)}, u32[]{:S(2)}) copy-start(f32[80,4096]{1,0:T(8,128)} %reduce_sum.96) | copy-start | bytes 3932164
Sparse Core Ops, SparseCore 0:
  59.9 148.0 all-gather.9
  210.2 123.1 all-gather.5
  335.4 123.1 all-gather.7
  460.7 7.2 reduce-scatter.2
  470.1 10.2 reduce-scatter.4
